TPU v7x, 32 devices: a whole 2x2x4 slice. The times are simulated.
32 devices in a mesh: group: 4 (over y, x), space: 8 (over z, core).
Axes of the slice: x: 2, y: 2, z: 4, core: 2. Of those that a mesh axis runs over, the one named last changes fastest.
Arguments:
- vectors: bfloat16 [128, 2, 3, 4096], P('group', None, None, 'space'), may hold values from -3 to 3
- momentum: int32 [3], replicated, may hold values from -3 to 3
- assignment: int32 [128], replicated, may hold values from 0 to 127, each once
Outputs:
- elementals: float32 [128, 2, 128, 128], P('space', None, 'group')
Inputs may be any that keep to these rules, and one draw needn't show every extreme that they name: `assignment`: each eigenvector is named by exactly one slot.
All inputs are finite; a program needn't handle non-finite values.
Results may differ from a plain program's by a relative error of at most 0.0029.
Values may be sent and summed in bfloat16 or wider, within the bound.
A program may use at most 128 MiB of HBM per device.

v0:
```python
import math
import jax
import jax.numpy as jnp
from jax import lax
from jax.sharding import PartitionSpec as P

L = 64


def complex_product(left_re, left_im, right_re, right_im):
    return (left_re * right_re - left_im * right_im, left_re * right_im + left_im * right_re)


def weighted_slot(vec32, slot_vec, cosine, sine):
    crosses_re = []
    crosses_im = []
    for colour in range(3):
        second = (colour + 1) % 3
        third = (colour + 2) % 3
        one_re, one_im = complex_product(
            vec32[:, 0, second], vec32[:, 1, second], slot_vec[0, third], slot_vec[1, third]
        )
        two_re, two_im = complex_product(
            vec32[:, 0, third], vec32[:, 1, third], slot_vec[0, second], slot_vec[1, second]
        )
        cross_re = one_re - two_re
        cross_im = one_im - two_im
        crosses_re.append(cross_re * cosine - cross_im * sine)
        crosses_im.append(cross_re * sine + cross_im * cosine)
    stacked = jnp.stack([jnp.stack(crosses_re, axis=1), jnp.stack(crosses_im, axis=1)], axis=1)
    return stacked.astype(jnp.bfloat16)


def local(vectors, momentum, assignment):
    block_size = vectors.shape[0]
    site_count = vectors.shape[3]
    space_size = lax.axis_size("space")
    total_sites = site_count * space_size
    gathered = lax.all_gather(vectors, "group", axis=0, tiled=True)
    total_vecs = gathered.shape[0]
    sites = lax.axis_index("space") * site_count + jnp.arange(site_count, dtype=jnp.int32)
    coord_x = sites % L
    coord_y = sites // L % L
    coord_z = sites // (L * L)
    phase_index = jnp.mod(momentum[0] * coord_x + momentum[1] * coord_y + momentum[2] * coord_z, L)
    angle = phase_index.astype(jnp.float32) * jnp.float32(2.0 * math.pi / L)
    cosine = jnp.cos(angle)
    sine = jnp.sin(angle)
    slot_ids = lax.dynamic_slice_in_dim(
        assignment, lax.axis_index("group") * block_size, block_size
    )
    vec32 = gathered.astype(jnp.float32)

    def one_slot(index):
        slot_vec = jnp.take(vec32, index, axis=0)
        return weighted_slot(vec32, slot_vec, cosine, sine)

    weighted = lax.map(one_slot, slot_ids).reshape(block_size * total_vecs, 2, 3 * site_count)
    flat_left = gathered.reshape(total_vecs, 2, 3 * site_count)
    scale = jnp.float32(1.0 / math.sqrt(total_sites))
    row_count = total_vecs // space_size
    products = jnp.einsum("ipx,mqx->ipqm", flat_left, weighted, preferred_element_type=jnp.float32)
    real_part = products[:, 0, 0] - products[:, 1, 1]
    imag_part = products[:, 0, 1] + products[:, 1, 0]
    joined = jnp.stack([real_part, imag_part], axis=1)
    summed = lax.psum(joined.reshape(total_vecs, 2, block_size, total_vecs) * scale, "space")
    return lax.dynamic_slice_in_dim(summed, lax.axis_index("space") * row_count, row_count, 0)


def solution(mesh):
    placed = (P("group", None, None, "space"), P(), P())
    return jax.shard_map(
        local,
        mesh=mesh,
        in_specs=placed,
        out_specs=P("space", None, "group", None),
        check_vma=False,
    )
```

profile of v0, /device:TPU:0, one launch (start us, length us, event | category | flops | bytes accessed | tf_op | source)
XLA Modules:
  0.0 420.4 jit_solution(16571338819917680055)
XLA Ops:
  6.5 13.9 %all_gather.3 = bf16[128,2,3,512]{3,1,2,0:T(2,128)(2,1)S(1)} all-gather(bf16[32,2,3,512]{3,1,2,0:T(2,128)(2,1)} %param.5), channel_id=1, replica_groups=mesh['group'=4,'space'=8] {'group'}, dimensions={0}, use_global_device_ids=true | all-gather | bytes 983040 | tf_op jit(solution)/shard_map/all_gather | solution.py:39
  22.3 197.2 %while.13 = (s32[]{:T(128)}, bf16[32,128,2,3,512]{4,1,3,2,0:T(8,128)(2,1)}, f32[128,2,3,512]{3,0,2,1:T(8,128)S(1)}, s32[32]{0:T(128)S(1)}, s32[]{:T(128)}, /*ind...) while((s32[]{:T(128)}, ...), condition=%wide.region_1.2_spmd.clone.clone, body=%wide.region_0.1_spmd.clone.clone.sunk | while | flops 6717960 | bytes 9810637 | solution.py:58
  24.6 2.1 fusion.48
  30.8 2.1 fusion.48
  33.6 1.0 maximum_dynamic-update-slice_fusion.2
  36.9 2.1 fusion.48
  43.1 2.1 fusion.48
  49.2 2.1 fusion.48
  55.4 2.1 fusion.48
  58.2 1.0 maximum_dynamic-update-slice_fusion.2
  61.5 2.1 fusion.48
  64.3 1.0 maximum_dynamic-update-slice_fusion.2
  67.7 2.1 fusion.48
  73.8 2.1 fusion.48
  76.7 1.0 maximum_dynamic-update-slice_fusion.2
  80.0 2.1 fusion.48
  86.1 2.1 fusion.48
  89.0 1.1 maximum_dynamic-update-slice_fusion.2
  92.4 2.1 fusion.48
  95.2 1.1 maximum_dynamic-update-slice_fusion.2
  98.6 2.1 fusion.48
  104.7 2.1 fusion.48
  107.6 1.0 maximum_dynamic-update-slice_fusion.2
  110.9 2.1 fusion.48
  113.7 1.0 maximum_dynamic-update-slice_fusion.2
  117.1 2.1 fusion.48
  119.9 1.0 maximum_dynamic-update-slice_fusion.2
  123.2 2.1 fusion.48
  126.1 1.0 maximum_dynamic-update-slice_fusion.2
  129.4 2.1 fusion.48
  135.6 2.1 fusion.48
  138.4 1.0 maximum_dynamic-update-slice_fusion.2
  141.8 2.1 fusion.48
  144.6 1.0 maximum_dynamic-update-slice_fusion.2
  147.9 2.1 fusion.48
  150.7 1.0 maximum_dynamic-update-slice_fusion.2
  154.1 2.1 fusion.48
  156.9 1.0 maximum_dynamic-update-slice_fusion.2
  160.2 2.1 fusion.48
  163.1 1.0 maximum_dynamic-update-slice_fusion.2
  166.4 2.1 fusion.48
  169.2 1.0 maximum_dynamic-update-slice_fusion.2
  172.6 2.1 fusion.48
  178.7 2.1 fusion.48
  181.5 1.0 maximum_dynamic-update-slice_fusion.2
  184.8 2.1 fusion.48
  191.0 2.1 fusion.48
  193.8 1.0 maximum_dynamic-update-slice_fusion.2
  197.1 2.1 fusion.48
  200.0 1.0 maximum_dynamic-update-slice_fusion.2
  203.3 2.1 fusion.48
  206.1 1.0 maximum_dynamic-update-slice_fusion.2
  209.5 2.1 fusion.48
  215.6 2.1 fusion.48
  218.4 1.0 maximum_dynamic-update-slice_fusion.2
  219.5 33.5 %copy.33 = bf16[32,128,2,3,512]{1,0,4,3,2:T(8,128)(2,1)} copy(bf16[32,128,2,3,512]{4,1,3,2,0:T(8,128)(2,1)} %get-tuple-element.37) | data formatting | bytes 50331648 | tf_op jit(solution)/shard_map/while | solution.py:58
  253.0 37.4 %reshape.2091 = bf16[4096,2,1536,1]{0,2,3,1:T(8,128)(2,1)} reshape(bf16[32,128,2,3,512]{1,0,4,3,2:T(8,128)(2,1)} %copy.33) | data formatting | bytes 50331648 | tf_op jit(solution)/shard_map/reshape | solution.py:58
  290.3 12.7 %convolution_bitcast_fusion = f32[128,2,2,4096]{0,3,1,2:T(8,128)S(1)} fusion(bf16[4096,2,1536,1]{0,2,3,1:T(8,128)(2,1)} %reshape.2091, bf16[128,2,1536,1]{0,2,1,3:T(8,128)(2,1)S(1)} %bitcast.179), kind=kOutput, calls=%fused_computation.85 | convolution fusion | flops 6442450944 | bytes 34340864 | tf_op jit(solution)/shard_map/ipx,mqx->ipqm/dot_general | solution.py:62
  303.0 1.8 slice_subtract_fusion
  304.8 3.2 copy.37
  307.9 2.0 copy.38
  310.0 4.8 %maximum_multiply_fusion = f32[128,2,32,128]{3,2,1,0:T(8,128)} fusion(f32[128,1,32,128]{3,2,1,0:T(8,128)} %copy.38, f32[128,1,32,128]{3,2,1,0:T(8,128)} %copy.37), kind=kLoop, calls=%fused_computation.86 | loop fusion | flops 2097152 | bytes 8388608 | tf_op jit(solution)/shard_map/mul | solution.py:66
  314.8 96.9 %all-reduce.2.cloned.1.call-done = f32[128,2,32,128]{3,2,1,0:T(8,128)} async-done(((f32[128,2,32,128]{3,2,1,0:T(8,128)}), f32[128,2,32,128]{3,2,1,0:T(8,128)}) %all-reduce.2.cloned.1.call-update) | async-done | bytes 4194320 | tf_op jit(solution)/shard_map/psum | solution.py:66
  411.7 1.9 constant_dynamic-slice_fusion
  (310 shorter events, 55.4 us)
Async XLA Ops:
  6.5 15.0 %copy-start = (s32[3]{0:T(128)S(1)}, s32[3]{0:T(128)}, u32[]{:S(2)}) copy-start(s32[3]{0:T(128)} %param.6) | copy-start | bytes 40
  6.5 15.7 %copy-start.1 = (s32[128]{0:T(128)S(1)}, s32[128]{0:T(128)}, u32[]{:S(2)}) copy-start(s32[128]{0:T(128)} %param.7) | copy-start | bytes 1540
  6.5 405.2 %all-reduce.2.cloned.1.call-start = ((), (), s32[]{:S(2)}) async-start(), calls=%async_computation | async-start | bytes 8388608 | tf_op jit(solution)/shard_map/psum | solution.py:66
Sparse Core Ops, SparseCore 0:
  314.9 96.7 all-reduce.1
where the time goes:
time: 424 us; the launch traced here: 420 us
  other arithmetic  129 us (30%)
  local copies, waits for them, and re-layouts  98.1 us (23%)
  waiting for transfers between devices  97 us (23%)
  loops' own time  56.6 us (13%)
  blocking collectives  13.9 us (3%)
  between operations  13.4 us (3%)
  matrix products  12.7 us (3%)
    psum x1, waiting for transfers between devices, local(): lax.psum(joined.reshape(total_vecs, 2, block_size, total_vecs) * scale, '...  96.9 us
    sin x32, other arithmetic, local(): sine = jnp.sin(angle)  65.9 us
    another operation x1, loops' own time, local(): lax.map(one_slot, slot_ids)  56.6 us
    reshape x1, local copies, waits for them, and re-layouts, local(): lax.map(one_slot, slot_ids)  37.4 us
    while x1, local copies, waits for them, and re-layouts, local(): lax.map(one_slot, slot_ids)  33.5 us
    dynamic_update_slice x32, other arithmetic, local(): lax.map(one_slot, slot_ids)  31.7 us
    another operation x96, other arithmetic  20.9 us
    dynamic_slice x32, local copies, waits for them, and re-layouts, local(): lax.map(one_slot, slot_ids)  17.8 us
  transfers between devices with their start and end apart: 1, of which 1 were waited for; matrix products, arithmetic and copies ran while one was open for 0% of the time, Pallas kernels for 0%

commit v1 on v0

--- a/solution.py
+++ b/solution.py
@@ -36,7 +36,26 @@
     site_count = vectors.shape[3]
     space_size = lax.axis_size("space")
     total_sites = site_count * space_size
-    gathered = lax.all_gather(vectors, "group", axis=0, tiled=True)
+    lower, front, arr_next = (
+        jax.lax.axis_size("group"),
+        jax.lax.axis_index("group"),
+        vectors.shape[0],
+    )
+    formed, main = (vectors, 1)
+    while main < lower:
+        formed = jnp.concatenate(
+            [
+                formed,
+                jax.lax.ppermute(
+                    formed,
+                    "group",
+                    tuple(((dev_j, (dev_j - main) % lower) for dev_j in range(lower))),
+                ),
+            ],
+            axis=0,
+        )
+        main = 2 * main
+    gathered = jnp.roll(formed, front * arr_next, 0)
     total_vecs = gathered.shape[0]
     sites = lax.axis_index("space") * site_count + jnp.arange(site_count, dtype=jnp.int32)
     coord_x = sites % L

time: 424 us -> 440 us (1.038)
  blocking collectives: 13.9 us -> 0 us
  waiting for transfers between devices: 97 us -> 108 us
  local copies, waits for them, and re-layouts: 98.1 us -> 109 us
  starting transfers between devices: 0.01 us -> 5.57 us
  loops' own time: 56.6 us -> 61.5 us
    all_gather x1 -> x0, blocking collectives: 13.9 us -> none  [local(): gathered = lax.all_gather(vectors, 'group', axis=0, tiled=True)]
    ppermute x0 -> x2, waiting for transfers between devices: none -> 8.81 us  [local(): jax.lax.ppermute(formed, 'group', tuple(((dev_j, (dev_j - main) % lower)...]
    ppermute x0 -> x2, starting transfers between devices: none -> 5.57 us  [local(): jax.lax.ppermute(formed, 'group', tuple(((dev_j, (dev_j - main) % lower)...]
    another operation x1, loops' own time: 56.6 us -> 61.5 us  [local(): lax.map(one_slot, slot_ids)]
  transfers between devices with their start and end apart: 1 -> 3, of which waited for: 1 -> 3; matrix products, arithmetic and copies ran while one was open for 0% -> 1% of each run, Pallas kernels for 0% -> 0%
where the time goes in v1:
time: 440 us; the launch traced here: 436 us
  other arithmetic  126 us (29%)
  local copies, waits for them, and re-layouts  109 us (25%)
  waiting for transfers between devices  108 us (25%)
  loops' own time  61.5 us (14%)
  between operations  13.5 us (3%)
  matrix products  12.7 us (3%)
  starting transfers between devices  5.57 us (1%)
    psum x1, waiting for transfers between devices, local(): lax.psum(joined.reshape(total_vecs, 2, block_size, total_vecs) * scale, '...  99 us
    sin x32, other arithmetic, local(): sine = jnp.sin(angle)  63 us
    another operation x1, loops' own time, local(): lax.map(one_slot, slot_ids)  61.5 us
    reshape x1, local copies, waits for them, and re-layouts, local(): lax.map(one_slot, slot_ids)  37.4 us
    while x1, local copies, waits for them, and re-layouts, local(): lax.map(one_slot, slot_ids)  33.5 us
    dynamic_update_slice x32, other arithmetic, local(): lax.map(one_slot, slot_ids)  31.7 us
    another operation x96, other arithmetic  20.9 us
    dynamic_slice x32, local copies, waits for them, and re-layouts, local(): lax.map(one_slot, slot_ids)  20.3 us
  transfers between devices with their start and end apart: 3, of which 3 were waited for; matrix products, arithmetic and copies ran while one was open for 1% of the time, Pallas kernels for 0%

profile of v1, /device:TPU:0, one launch (start us, length us, event | category | flops | bytes accessed | tf_op | source)
XLA Modules:
  0.0 436.1 jit_solution(4805674354528777546)
XLA Ops:
  7.5 3.9 collective-permute-start
  11.4 4.2 collective-permute-done
  15.6 1.6 collective-permute-start.1
  17.3 1.3 copy.52
  19.3 1.4 fusion.43
  21.1 4.7 %collective-permute-done.1 = bf16[64,2,3,512]{3,0,2,1:T(8,128)(2,1)S(1)} collective-permute-done((bf16[64,2,3,512]{3,0,2,1:T(8,128)(2,1)S(1)}, bf16[64,2,3,512]{3,0,2,1:T(8,128)(2,1)S(1)}, u32[]{:S(2)}, u32[]{:S(2)}) %collective-permute-start.1) | collective-permute-done | bytes 393248 | tf_op jit(solution)/shard_map/ppermute | solution.py:49
  26.2 3.4 concatenate.20
  29.6 1.4 constant_dynamic-slice_fusion.1
  31.3 201.7 %while.13 = (s32[]{:T(128)}, bf16[32,128,2,3,512]{4,1,3,2,0:T(8,128)(2,1)}, f32[128,2,3,512]{3,0,2,1:T(8,128)S(1)}, s32[32]{0:T(128)S(1)}, s32[]{:T(128)}, /*ind...) while((s32[]{:T(128)}, ...), condition=%wide.region_1.2_spmd.clone.clone, body=%wide.region_0.1_spmd.clone.clone.sunk | while | flops 6717960 | bytes 9810637 | solution.py:77
  33.9 2.0 fusion.48
  40.2 2.0 fusion.48
  42.9 1.0 maximum_dynamic-update-slice_fusion.2
  46.5 2.0 fusion.48
  52.7 2.0 fusion.48
  59.0 2.0 fusion.48
  65.3 2.0 fusion.48
  71.6 2.0 fusion.48
  74.4 1.0 maximum_dynamic-update-slice_fusion.2
  77.9 2.0 fusion.48
  84.2 2.0 fusion.48
  90.5 2.0 fusion.48
  96.8 2.0 fusion.48
  99.5 1.1 maximum_dynamic-update-slice_fusion.2
  103.2 2.0 fusion.48
  105.9 1.1 maximum_dynamic-update-slice_fusion.2
  109.6 2.0 fusion.48
  115.8 2.0 fusion.48
  118.6 1.0 maximum_dynamic-update-slice_fusion.2
  122.1 2.0 fusion.48
  128.4 2.0 fusion.48
  131.2 1.0 maximum_dynamic-update-slice_fusion.2
  134.8 2.0 fusion.48
  137.5 1.0 maximum_dynamic-update-slice_fusion.2
  141.1 2.0 fusion.48
  147.4 2.0 fusion.48
  150.1 1.0 maximum_dynamic-update-slice_fusion.2
  153.7 2.0 fusion.48
  156.4 1.0 maximum_dynamic-update-slice_fusion.2
  160.0 2.0 fusion.48
  162.7 1.0 maximum_dynamic-update-slice_fusion.2
  166.3 2.0 fusion.48
  172.6 2.0 fusion.48
  178.9 2.0 fusion.48
  181.6 1.0 maximum_dynamic-update-slice_fusion.2
  185.2 2.0 fusion.48
  191.5 2.0 fusion.48
  197.8 2.0 fusion.48
  204.0 2.0 fusion.48
  210.3 2.0 fusion.48
  213.1 1.0 maximum_dynamic-update-slice_fusion.2
  216.6 2.0 fusion.48
  219.4 1.0 maximum_dynamic-update-slice_fusion.2
  222.9 2.0 fusion.48
  229.2 2.0 fusion.48
  232.0 1.0 maximum_dynamic-update-slice_fusion.2
  233.0 33.5 %copy.59 = bf16[32,128,2,3,512]{1,0,4,3,2:T(8,128)(2,1)} copy(bf16[32,128,2,3,512]{4,1,3,2,0:T(8,128)(2,1)} %get-tuple-element.37) | data formatting | bytes 50331648 | tf_op jit(solution)/shard_map/while | solution.py:77
  266.5 37.4 %reshape.2091 = bf16[4096,2,1536,1]{0,2,3,1:T(8,128)(2,1)} reshape(bf16[32,128,2,3,512]{1,0,4,3,2:T(8,128)(2,1)} %copy.59) | data formatting | bytes 50331648 | tf_op jit(solution)/shard_map/reshape | solution.py:77
  303.9 12.7 %convolution_bitcast_fusion = f32[128,2,2,4096]{0,3,1,2:T(8,128)S(1)} fusion(bf16[4096,2,1536,1]{0,2,3,1:T(8,128)(2,1)} %reshape.2091, bf16[128,2,1536,1]{0,2,1,3:T(8,128)(2,1)S(1)} %bitcast.178), kind=kOutput, calls=%fused_computation.85 | convolution fusion | flops 6442450944 | bytes 34340864 | tf_op jit(solution)/shard_map/ipx,mqx->ipqm/dot_general | solution.py:81
  316.6 1.8 slice_subtract_fusion
  318.3 3.2 copy.62
  321.5 2.0 copy.63
  323.5 4.8 %maximum_multiply_fusion = f32[128,2,32,128]{3,2,1,0:T(8,128)} fusion(f32[128,1,32,128]{3,2,1,0:T(8,128)} %copy.63, f32[128,1,32,128]{3,2,1,0:T(8,128)} %copy.62), kind=kLoop, calls=%fused_computation.86 | loop fusion | flops 2097152 | bytes 8388608 | tf_op jit(solution)/shard_map/mul | solution.py:85
  328.3 99.0 %all-reduce.2.cloned.1.call-done = f32[128,2,32,128]{3,2,1,0:T(8,128)} async-done(((f32[128,2,32,128]{3,2,1,0:T(8,128)}), f32[128,2,32,128]{3,2,1,0:T(8,128)}) %all-reduce.2.cloned.1.call-update) | async-done | bytes 4194320 | tf_op jit(solution)/shard_map/psum | solution.py:85
  427.4 1.9 constant_dynamic-slice_fusion
  (315 shorter events, 65.8 us)
Async XLA Ops:
  6.5 420.8 %all-reduce.2.cloned.1.call-start = ((), (), s32[]{:S(2)}) async-start(), calls=%async_computation | async-start | bytes 8388608 | tf_op jit(solution)/shard_map/psum | solution.py:85
  7.5 8.1 %collective-permute-start = (bf16[32,2,3,512]{3,0,2,1:T(8,128)(2,1)S(1)}, bf16[32,2,3,512]{3,0,2,1:T(8,128)(2,1)S(1)}, u32[]{:S(2)}, u32[]{:S(2)}) collective-permute-start(bf16[32,2,3,512]{3,0,2,1:T(8,128)(2,1)S(1)} %copy.50), channel_id=1, source_target_pairs={{0,24},{8,0},{16,8},{24,16},{1,25},{9,1},{17,9},{25,17},{2,26},{10... | collective-permute-start | bytes 589832 | tf_op jit(solution)/shard_map/ppermute | solution.py:49
  15.6 10.2 %collective-permute-start.1 = (bf16[64,2,3,512]{3,0,2,1:T(8,128)(2,1)S(1)}, bf16[64,2,3,512]{3,0,2,1:T(8,128)(2,1)S(1)}, u32[]{:S(2)}, u32[]{:S(2)}) collective-permute-start(bf16[64,2,3,512]{3,0,2,1:T(8,128)(2,1)S(1)} %pad_maximum_fusion), channel_id=1, source_target_pairs={{0,16},{8,24},{16,0},{24,8},{1,17},{9,25},{17,1},{25,9},{2,18},{10... | collective-permute-start | bytes 1179656 | tf_op jit(solution)/shard_map/ppermute | solution.py:49
Sparse Core Ops, SparseCore 0:
  328.4 98.8 all-reduce.1

commit v2 on v0

--- a/solution.py
+++ b/solution.py
@@ -63,7 +63,9 @@
     real_part = products[:, 0, 0] - products[:, 1, 1]
     imag_part = products[:, 0, 1] + products[:, 1, 0]
     joined = jnp.stack([real_part, imag_part], axis=1)
-    summed = lax.psum(joined.reshape(total_vecs, 2, block_size, total_vecs) * scale, "space")
+    own = joined.reshape(total_vecs, 2, block_size, total_vecs) * scale
+    blocks = lax.all_gather(own, "space")
+    summed = jnp.sum(blocks, axis=0)
     return lax.dynamic_slice_in_dim(summed, lax.axis_index("space") * row_count, row_count, 0)
 
 

time: 424 us -> 631 us (1.49)
  waiting for transfers between devices: 97 us -> 289 us
  other arithmetic: 129 us -> 144 us
    all_gather x0 -> x1, waiting for transfers between devices: none -> 289 us  [local(): blocks = lax.all_gather(own, 'space')]
    psum x1 -> x0, waiting for transfers between devices: 96.9 us -> none  [local(): lax.psum(joined.reshape(total_vecs, 2, block_size, total_vecs) * scale, '...]
    reduce_sum x0 -> x1, other arithmetic: none -> 15.2 us  [local(): summed = jnp.sum(blocks, axis=0)]
where the time goes in v2:
time: 631 us; the launch traced here: 628 us
  waiting for transfers between devices  289 us (46%)
  other arithmetic  144 us (23%)
  local copies, waits for them, and re-layouts  98.1 us (16%)
  loops' own time  56.6 us (9%)
  blocking collectives  13.9 us (2%)
  between operations  13.4 us (2%)
  matrix products  12.7 us (2%)
    all_gather x1, waiting for transfers between devices, local(): blocks = lax.all_gather(own, 'space')  289 us
    sin x32, other arithmetic, local(): sine = jnp.sin(angle)  65.9 us
    another operation x1, loops' own time, local(): lax.map(one_slot, slot_ids)  56.6 us
    reshape x1, local copies, waits for them, and re-layouts, local(): lax.map(one_slot, slot_ids)  37.4 us
    while x1, local copies, waits for them, and re-layouts, local(): lax.map(one_slot, slot_ids)  33.5 us
    dynamic_update_slice x32, other arithmetic, local(): lax.map(one_slot, slot_ids)  31.7 us
    another operation x96, other arithmetic  20.9 us
    dynamic_slice x32, local copies, waits for them, and re-layouts, local(): lax.map(one_slot, slot_ids)  17.8 us
  transfers between devices with their start and end apart: 1, of which 1 were waited for; matrix products, arithmetic and copies ran while one was open for 0% of the time, Pallas kernels for 0%

profile of v2, /device:TPU:0, one launch (start us, length us, event | category | flops | bytes accessed | tf_op | source)
XLA Modules:
  0.0 627.8 jit_solution(8605753754241394115)
XLA Ops:
  6.5 13.9 %all_gather.7 = bf16[128,2,3,512]{3,1,2,0:T(2,128)(2,1)S(1)} all-gather(bf16[32,2,3,512]{3,1,2,0:T(2,128)(2,1)} %param.5), channel_id=1, replica_groups=mesh['group'=4,'space'=8] {'group'}, dimensions={0}, use_global_device_ids=true | all-gather | bytes 983040 | tf_op jit(solution)/shard_map/all_gather | solution.py:39
  22.3 197.2 %while.13 = (s32[]{:T(128)}, bf16[32,128,2,3,512]{4,1,3,2,0:T(8,128)(2,1)}, f32[128,2,3,512]{3,0,2,1:T(8,128)S(1)}, s32[32]{0:T(128)S(1)}, s32[]{:T(128)}, /*ind...) while((s32[]{:T(128)}, ...), condition=%wide.region_1.2_spmd.clone.clone, body=%wide.region_0.1_spmd.clone.clone.sunk | while | flops 6717960 | bytes 9810637 | solution.py:58
  24.6 2.1 fusion.48
  30.8 2.1 fusion.48
  33.6 1.0 maximum_dynamic-update-slice_fusion.2
  36.9 2.1 fusion.48
  43.1 2.1 fusion.48
  49.2 2.1 fusion.48
  55.4 2.1 fusion.48
  58.2 1.0 maximum_dynamic-update-slice_fusion.2
  61.5 2.1 fusion.48
  64.3 1.0 maximum_dynamic-update-slice_fusion.2
  67.7 2.1 fusion.48
  73.8 2.1 fusion.48
  76.7 1.0 maximum_dynamic-update-slice_fusion.2
  80.0 2.1 fusion.48
  86.1 2.1 fusion.48
  89.0 1.1 maximum_dynamic-update-slice_fusion.2
  92.4 2.1 fusion.48
  95.2 1.1 maximum_dynamic-update-slice_fusion.2
  98.6 2.1 fusion.48
  104.7 2.1 fusion.48
  107.6 1.0 maximum_dynamic-update-slice_fusion.2
  110.9 2.1 fusion.48
  113.7 1.0 maximum_dynamic-update-slice_fusion.2
  117.1 2.1 fusion.48
  119.9 1.0 maximum_dynamic-update-slice_fusion.2
  123.2 2.1 fusion.48
  126.1 1.0 maximum_dynamic-update-slice_fusion.2
  129.4 2.1 fusion.48
  135.6 2.1 fusion.48
  138.4 1.0 maximum_dynamic-update-slice_fusion.2
  141.8 2.1 fusion.48
  144.6 1.0 maximum_dynamic-update-slice_fusion.2
  147.9 2.1 fusion.48
  150.7 1.0 maximum_dynamic-update-slice_fusion.2
  154.1 2.1 fusion.48
  156.9 1.0 maximum_dynamic-update-slice_fusion.2
  160.2 2.1 fusion.48
  163.1 1.0 maximum_dynamic-update-slice_fusion.2
  166.4 2.1 fusion.48
  169.2 1.0 maximum_dynamic-update-slice_fusion.2
  172.6 2.1 fusion.48
  178.7 2.1 fusion.48
  181.5 1.0 maximum_dynamic-update-slice_fusion.2
  184.8 2.1 fusion.48
  191.0 2.1 fusion.48
  197.1 2.1 fusion.48
  200.0 1.0 maximum_dynamic-update-slice_fusion.2
  203.3 2.1 fusion.48
  206.1 1.0 maximum_dynamic-update-slice_fusion.2
  209.5 2.1 fusion.48
  215.6 2.1 fusion.48
  218.4 1.0 maximum_dynamic-update-slice_fusion.2
  219.5 33.5 %copy.33 = bf16[32,128,2,3,512]{1,0,4,3,2:T(8,128)(2,1)} copy(bf16[32,128,2,3,512]{4,1,3,2,0:T(8,128)(2,1)} %get-tuple-element.37) | data formatting | bytes 50331648 | tf_op jit(solution)/shard_map/while | solution.py:58
  253.0 37.4 %reshape.2134 = bf16[4096,2,1536,1]{0,2,3,1:T(8,128)(2,1)} reshape(bf16[32,128,2,3,512]{1,0,4,3,2:T(8,128)(2,1)} %copy.33) | data formatting | bytes 50331648 | tf_op jit(solution)/shard_map/reshape | solution.py:58
  290.3 12.7 %convolution_bitcast_fusion = f32[128,2,2,4096]{0,3,1,2:T(8,128)S(1)} fusion(bf16[4096,2,1536,1]{0,2,3,1:T(8,128)(2,1)} %reshape.2134, bf16[128,2,1536,1]{0,2,1,3:T(8,128)(2,1)S(1)} %bitcast.179), kind=kOutput, calls=%fused_computation.85 | convolution fusion | flops 6442450944 | bytes 34340864 | tf_op jit(solution)/shard_map/ipx,mqx->ipqm/dot_general | solution.py:62
  303.0 1.7 slice_subtract_fusion
  304.8 3.1 copy.37
  307.9 2.0 copy.38
  309.9 4.9 maximum_multiply_fusion
  314.8 289.0 %all-gather.2.cloned.1.call-done = f32[8,128,2,32,128]{4,3,2,1,0:T(8,128)} async-done(((f32[1,128,2,32,128]{4,3,2,1,0:T(8,128)}), f32[8,128,2,32,128]{4,3,2,1,0:T(8,128)}) %all-gather.2.cloned.1.call-update) | async-done | bytes 33554448 | tf_op jit(solution)/shard_map/all_gather | solution.py:67
  603.9 15.2 %reduce_sum.9 = f32[128,2,32,128]{3,2,1,0:T(8,128)} reduce(f32[8,128,2,32,128]{4,3,2,1,0:T(8,128)} %all-gather.2.cloned.1.call-done, f32[]{:T(128)} %constant.95.clone.1), dimensions={0}, to_apply=%region_2.3 | reduce | flops 7340032 | bytes 37748740 | tf_op jit(solution)/shard_map/reduce_sum | solution.py:68
  619.0 1.9 constant_dynamic-slice_fusion
  (311 shorter events, 56.4 us)
Async XLA Ops:
  6.5 15.0 %copy-start = (s32[3]{0:T(128)S(1)}, s32[3]{0:T(128)}, u32[]{:S(2)}) copy-start(s32[3]{0:T(128)} %param.6) | copy-start | bytes 40
  6.5 15.7 %copy-start.1 = (s32[128]{0:T(128)S(1)}, s32[128]{0:T(128)}, u32[]{:S(2)}) copy-start(s32[128]{0:T(128)} %param.7) | copy-start | bytes 1540
  6.5 597.3 %all-gather.2.cloned.1.call-start = ((), (), s32[]{:S(2)}) async-start(), calls=%async_computation | async-start | bytes 37748736 | tf_op jit(solution)/shard_map/all_gather | solution.py:67
Sparse Core Ops, SparseCore 0:
  315.0 288.8 all-gather.1
